TPU v7x, 256 devices: a whole 4x4x8 slice. The times are simulated.
256 devices in a mesh: row: 16 (over y, x), col: 16 (over z, core).
Axes of the slice: x: 4, y: 4, z: 8, core: 2. Of those that a mesh axis runs over, the one named last changes fastest.
Arguments:
- fitting: bfloat16 [512, 512, 256], P(('row', 'col')), may hold values from -6 to 6
- coefficients: bfloat16 [64, 64, 6, 256, 128], P('row', 'col'), may hold values from -0.375 to 0.375
- amplitudes: bfloat16 [64, 64, 4096], P('row', 'col'), may hold values from -6 to 6
- intersections: bfloat16 [64, 64, 8, 4096], P('row', 'col'), may hold values from -0.33 to 1.33
- virtual_energy: float32 [64, 64, 64], P('row', 'col'), may hold values from 0.2 to 2
- occupied_energy: float32 [64], replicated, may hold values from -1.5 to -0.3
- kept_count: int32 [64, 64], P('row', 'col'), may hold values from 16 to 64
- orbital_atoms: int32 [64, 3], replicated, may hold values from 0 to 511, as said below
- fock_partner: int32 [64, 4], replicated, may hold values from 0 to 63, as said below
- fock_value: float32 [64, 4], replicated, may hold values from -3 to 3
Outputs:
- residual: float32 [64, 64, 4096], P('row', 'col')
Inputs may be any that keep to these rules, and one draw needn't show every extreme that they name: `orbital_atoms`: the 3 atoms of orbital i are different and lie in [(i // 4) * 32, (i // 4 + 1) * 32). fock_partner[i, n] differs from i by at most 4.
All inputs are finite; a program needn't handle non-finite values.
Results may differ from a plain program's by a relative error of at most 0.0029.
Values may be sent and summed in bfloat16 or wider, within the bound.
A program may use at most 128 MiB of HBM per device.

v0:
```python
import jax
import jax.numpy as jnp
from jax import lax
from jax.sharding import PartitionSpec as P

AUX = 512
NPNO = 64
DOMAIN = 3
PARTNERS = 4


def from_root(value, axis, source):
    kept = jnp.where(lax.axis_index(axis) == source, value, 0).astype(value.dtype)
    return lax.psum(kept, axis)


def passed_along(block, axis, distance):
    devices = range(lax.axis_size(axis))
    route = [(i - distance, i) for i in devices if i - distance in devices]
    return lax.ppermute(block, axis, route)


def on_device(
    fitting,
    coefficients,
    amplitudes,
    intersections,
    virtual_energy,
    occupied_energy,
    kept_count,
    orbital_atoms,
    fock_partner,
    fock_value,
):
    row_count = amplitudes.shape[0]
    column_count = amplitudes.shape[1]
    domain_size = orbital_atoms.shape[1]
    row_place = lax.axis_index("row")
    column_place = lax.axis_index("col")
    row_atoms = fitting.shape[0] * lax.axis_size("col")
    first_row = row_place * row_count
    first_column = column_place * column_count
    wanted = (
        lax.dynamic_slice_in_dim(orbital_atoms, first_row, row_count, 0) - row_place * row_atoms
    )
    piece = lax.all_gather(fitting, "col", axis=0, tiled=True)
    labels = jnp.arange(piece.shape[0], dtype=jnp.int32)
    picker = (wanted[:, :, None] == labels[None, None, :]).astype(jnp.bfloat16)
    added = jnp.einsum("ism,map->isap", picker, piece, preferred_element_type=jnp.float32)
    row_fit = added.astype(jnp.bfloat16)
    source_row = first_column // row_count
    column_fit = from_root(row_fit, "row", source_row)
    own_side = jnp.einsum(
        "isap,ijspq->ijsaq",
        row_fit,
        coefficients[:, :, :domain_size],
        preferred_element_type=jnp.float32,
    ).astype(jnp.bfloat16)
    other_side = jnp.einsum(
        "jsap,ijspq->ijsaq",
        column_fit,
        coefficients[:, :, domain_size:],
        preferred_element_type=jnp.float32,
    ).astype(jnp.bfloat16)
    exchange_part = jnp.einsum(
        "ijsaq,ijsar->ijqr",
        own_side[..., :NPNO],
        own_side[..., NPNO:],
        preferred_element_type=jnp.float32,
    )
    exchange_part = exchange_part + jnp.einsum(
        "ijsaq,ijsar->ijqr",
        other_side[..., :NPNO],
        other_side[..., NPNO:],
        preferred_element_type=jnp.float32,
    )
    exchange_part = exchange_part * (2 * DOMAIN * AUX) ** (-0.5)
    row_partner = lax.dynamic_slice_in_dim(fock_partner, first_row, row_count, 0)
    column_partner = lax.dynamic_slice_in_dim(fock_partner, first_column, column_count, 0)
    below_rows = passed_along(amplitudes, "row", 1)
    above_rows = passed_along(amplitudes, "row", -1)
    row_source = jnp.concatenate([below_rows, amplitudes, above_rows], axis=0)
    below_columns = passed_along(amplitudes, "col", 1)
    above_columns = passed_along(amplitudes, "col", -1)
    column_source = jnp.concatenate([below_columns, amplitudes, above_columns], axis=1)
    row_pick = row_partner - (first_row - column_count)
    column_pick = column_partner - (first_column - column_count)
    from_rows = jnp.transpose(jnp.take(row_source, row_pick, axis=0), (0, 2, 1, 3))
    from_columns = jnp.take(column_source, column_pick, axis=1)
    partners = jnp.concatenate([from_rows, from_columns], axis=2).reshape(
        row_count, column_count, 2 * PARTNERS, NPNO, NPNO
    )
    intersection_mats = intersections.reshape(row_count, column_count, 2 * PARTNERS, NPNO, NPNO)
    half = jnp.einsum(
        "ijnab,ijnbc->ijnac", intersection_mats, partners, preferred_element_type=jnp.float32
    ).astype(jnp.bfloat16)
    sandwich = jnp.einsum(
        "ijnac,ijndc->ijnad", half, intersection_mats, preferred_element_type=jnp.float32
    )
    row_weight = lax.dynamic_slice_in_dim(fock_value, first_row, row_count, 0)
    column_weight = lax.dynamic_slice_in_dim(fock_value, first_column, column_count, 0)
    weights = jnp.concatenate(
        [
            jnp.broadcast_to(row_weight[:, None, :], (row_count, column_count, PARTNERS)),
            jnp.broadcast_to(column_weight[None, :, :], (row_count, column_count, PARTNERS)),
        ],
        axis=2,
    )
    coupling = jnp.einsum("ijn,ijnad->ijad", weights, sandwich)
    row_occupied = lax.dynamic_slice_in_dim(occupied_energy, first_row, row_count, 0)
    column_occupied = lax.dynamic_slice_in_dim(occupied_energy, first_column, column_count, 0)
    shift = (
        virtual_energy[:, :, :, None]
        + virtual_energy[:, :, None, :]
        - row_occupied[:, None, None, None]
        - column_occupied[None, :, None, None]
    )
    current = amplitudes.reshape(row_count, column_count, NPNO, NPNO).astype(jnp.float32)
    result = exchange_part + shift * current - coupling
    levels = jnp.arange(NPNO, dtype=jnp.int32)
    count = kept_count[:, :, None, None]
    keep = (levels[None, None, :, None] < count) & (levels[None, None, None, :] < count)
    masked = jnp.where(keep, result, jnp.zeros_like(result))
    return masked.reshape(row_count, column_count, NPNO * NPNO)


def solution(mesh):
    placed = (
        P(("row", "col"), None, None),
        P("row", "col", None, None, None),
        P("row", "col", None),
        P("row", "col", None, None),
        P("row", "col", None),
        P(),
        P("row", "col"),
        P(),
        P(),
        P(),
    )
    return jax.shard_map(
        on_device, mesh=mesh, in_specs=placed, out_specs=P("row", "col", None), check_vma=False
    )
```

profile of v0, /device:TPU:1, one launch (start us, length us, event | category | flops | bytes accessed | tf_op | source)
XLA Modules:
  0.0 198.9 jit_solution(497864777100827050)
XLA Ops:
  6.5 0.7 all-gather.2.cloned.1.call-update
  7.3 0.0 all-reduce.2.cloned.1.call-start
  7.3 1.0 copy.82
  8.3 4.9 %collective-permute-start.2 = (bf16[4,4,4096]{2,0,1:T(4,128)(2,1)S(1)}, bf16[4,4,4096]{2,0,1:T(4,128)(2,1)S(1)}, u32[]{:S(2)}, u32[]{:S(2)}) collective-permute-start(bf16[4,4,4096]{2,0,1:T(4,128)(2,1)S(1)} %copy.82), channel_id=1, source_target_pairs={{0,1},{1,2},{2,3},{3,4},{4,5},{5,6},{6,7},{7,8},{8,9},{9,10},{10,1... | collective-permute-start | bytes 393224 | tf_op jit(solution)/shard_map/ppermute | solution.py:20
  13.2 1.9 collective-permute-start.3
  15.2 3.1 %collective-permute-start = (bf16[4,4,4096]{2,1,0:T(4,128)(2,1)}, bf16[4,4,4096]{2,1,0:T(4,128)(2,1)S(1)}, u32[]{:S(2)}, u32[]{:S(2)}) collective-permute-start(bf16[4,4,4096]{2,1,0:T(4,128)(2,1)} %param.12), channel_id=1, source_target_pairs={{0,16},{16,32},{32,48},{48,64},{64,80},{80,96},{96,112},{112,128},... | collective-permute-start | bytes 393224 | tf_op jit(solution)/shard_map/ppermute | solution.py:20
  18.3 1.3 collective-permute-start.1
  19.6 0.8 compare_and_fusion.1
  20.5 0.1 copy.85
  20.6 0.1 reshape.58
  20.6 0.1 copy.79
  20.7 0.1 reshape.50
  20.8 0.8 dynamic-slice_subtract_fusion
  21.6 0.8 constant_dynamic-slice_fusion.1
  22.4 0.8 iota_compare_fusion
  23.2 6.7 %fusion.63 = (bf16[4,4,3,256,128]{4,3,2,1,0:T(8,128)(2,1)}, bf16[4,4,3,256,128]{4,3,2,1,0:T(8,128)(2,1)}) fusion(bf16[4,4,6,256,128]{4,3,2,1,0:T(8,128)(2,1)} %param.11), kind=kLoop, calls=%fused_computation.53 | loop fusion | bytes 12582912 | tf_op jit(solution)/shard_map/slice | solution.py:62
  29.9 0.1 fusion.65
  30.0 1.0 reshape.47
  31.1 0.1 copy.81
  31.2 0.1 copy.78
  31.3 3.3 %reshape.45 = bf16[4,4,8,64,64]{4,3,2,1,0:T(8,128)(2,1)S(1)} reshape(bf16[4,4,8,4096]{3,2,1,0:T(8,128)(2,1)} %param.13) | data formatting | bytes 2097152 | tf_op jit(solution)/shard_map/reshape | solution.py:93
  34.5 0.1 copy.76
  34.6 0.1 copy.77
  34.7 0.1 pad_maximum_fusion.3
  34.8 0.3 pad_maximum_fusion.2
  35.1 1.0 gather_fusion.1
  36.1 0.3 pad_maximum_fusion.1
  36.4 1.8 gather_fusion
  38.2 1.5 fusion.57
  39.7 29.6 %all-gather.2.cloned.1.call-done = bf16[32,512,256]{2,1,0:T(8,128)(2,1)} async-done(((bf16[2,512,256]{2,1,0:T(8,128)(2,1)}), bf16[32,512,256]{2,1,0:T(8,128)(2,1)}) %all-gather.2.cloned.1.call-update) | async-done | bytes 8388624 | tf_op jit(solution)/shard_map/all_gather | solution.py:46
  69.2 12.0 %broadcast_select_fusion = (bf16[4,3,512,256]{3,0,2,1:T(4,128)(2,1)}, bf16[4,3,512,256]{3,0,2,1:T(4,128)(2,1)}) fusion(pred[]{:T(512)S(6)} %eq.19, bf16[32,512,256]{2,1,0:T(8,128)(2,1)} %all-gather.2.cloned.1.call-done, s32[4,3]{0,1:T(4,128)S(1)} %dynamic-slice_subtract_fusion), kind=kOutput, calls=%fused_computation.19 | convolution fusion | flops 103809408 | bytes 14680113 | tf_op jit(solution)/shard_map/ism,map->isap/dot_general | solution.py:49
  81.2 0.0 all-reduce.2.cloned.1.call-update
  81.2 2.0 pad_maximum_fusion
  83.2 3.3 %reshape.44 = bf16[4,4,8,64,64]{4,3,2,1,0:T(8,128)(2,1)} reshape(bf16[4,4,8,4096]{3,2,1,0:T(8,128)(2,1)S(1)} %pad_maximum_fusion) | data formatting | bytes 2097152 | tf_op jit(solution)/shard_map/reshape | solution.py:90
  86.5 5.3 %fusion.18 = bf16[4,4,8,64,64]{4,3,2,1,0:T(8,128)(2,1)} fusion(bf16[4,4,8,64,64]{4,3,2,1,0:T(8,128)(2,1)S(1)} %reshape.45, bf16[4,4,8,64,64]{4,3,2,1,0:T(8,128)(2,1)} %reshape.44), kind=kOutput, calls=%fused_computation.21 | convolution fusion | flops 134742016 | bytes 3145728 | tf_op jit(solution)/shard_map/ijnac,ijndc->ijnad/dot_general | solution.py:97
  91.8 3.8 %fusion.3 = f32[4,4,1,64,64]{4,2,3,1,0:T(1,128)} fusion(f32[4,4,8,1,1]{2,3,4,1,0:T(1,128)S(1)} %bitcast.64, bf16[4,4,8,64,64]{4,3,2,1,0:T(8,128)(2,1)} %fusion.18), kind=kOutput, calls=%fused_computation.7 | convolution fusion | flops 1048576 | bytes 1311232 | tf_op jit(solution)/shard_map/ijn,ijnad->ijad/dot_general | solution.py:109
  95.6 4.8 %convert_bitcast_fusion.1 = bf16[4,4,3,512,128]{3,4,1,2,0:T(8,128)(2,1)S(1)} fusion(bf16[4,4,3,256,128]{4,3,2,1,0:T(8,128)(2,1)} %get-tuple-element.12, bf16[4,3,512,256,1]{3,0,2,1,4:T(4,128)(2,1)} %bitcast.60), kind=kOutput, calls=%fused_computation.6 | convolution fusion | flops 1613758464 | bytes 12582912 | tf_op jit(solution)/shard_map/isap,ijspq->ijsaq/dot_general | solution.py:53
  100.4 0.8 fusion.64
  101.2 1.7 fusion.22
  103.0 82.1 %all-reduce.2.cloned.1.call-done = bf16[4,3,512,256]{3,0,2,1:T(4,128)(2,1)} async-done(((bf16[4,3,512,256]{3,0,2,1:T(4,128)(2,1)}), bf16[4,3,512,256]{3,0,2,1:T(4,128)(2,1)}) %all-reduce.2.cloned.1.call-update) | async-done | bytes 3145744 | tf_op jit(solution)/shard_map/psum | solution.py:14
  185.1 3.7 %convert_bitcast_fusion = bf16[4,4,3,512,128]{3,4,0,2,1:T(8,128)(2,1)S(1)} fusion(bf16[4,4,3,256,128]{4,3,2,1,0:T(8,128)(2,1)S(1)} %copy-done, bf16[4,3,512,256,1]{3,0,2,1,4:T(4,128)(2,1)} %bitcast.59), kind=kOutput, calls=%fused_computation.5 | convolution fusion | flops 1613758464 | bytes 12582912 | tf_op jit(solution)/shard_map/jsap,ijspq->ijsaq/dot_general | solution.py:59
  188.8 0.0 copy-start.5
  188.8 0.4 fusion.62
  189.3 0.5 copy-done.2
  189.8 0.2 copy-done.3
  190.0 0.2 copy-done.6
  190.2 1.0 fusion.52
  191.2 0.9 reshape.46
  (19 shorter events, 0.0 us)
Async XLA Ops:
  6.5 62.7 %all-gather.2.cloned.1.call-start = ((), (), s32[]{:S(2)}) async-start(), calls=%async_computation | async-start | bytes 8912896 | tf_op jit(solution)/shard_map/all_gather | solution.py:46
  7.3 177.8 %all-reduce.2.cloned.1.call-start = ((), (), s32[]{:S(2)}) async-start(), calls=%async_computation.1 | async-start | bytes 6291456 | tf_op jit(solution)/shard_map/psum | solution.py:14
  8.3 26.5 %collective-permute-start.2 = (bf16[4,4,4096]{2,0,1:T(4,128)(2,1)S(1)}, bf16[4,4,4096]{2,0,1:T(4,128)(2,1)S(1)}, u32[]{:S(2)}, u32[]{:S(2)}) collective-permute-start(bf16[4,4,4096]{2,0,1:T(4,128)(2,1)S(1)} %copy.82), channel_id=1, source_target_pairs={{0,1},{1,2},{2,3},{3,4},{4,5},{5,6},{6,7},{7,8},{8,9},{9,10},{10,1... | collective-permute-start | bytes 393224 | tf_op jit(solution)/shard_map/ppermute | solution.py:20
  13.2 21.6 %collective-permute-start.3 = (bf16[4,4,4096]{2,0,1:T(4,128)(2,1)S(1)}, bf16[4,4,4096]{2,0,1:T(4,128)(2,1)S(1)}, u32[]{:S(2)}, u32[]{:S(2)}) collective-permute-start(bf16[4,4,4096]{2,0,1:T(4,128)(2,1)S(1)} %copy.82), channel_id=1, source_target_pairs={{1,0},{2,1},{3,2},{4,3},{5,4},{6,5},{7,6},{8,7},{9,8},{10,9},{11,1... | collective-permute-start | bytes 393224 | tf_op jit(solution)/shard_map/ppermute | solution.py:20
  15.2 20.9 %collective-permute-start = (bf16[4,4,4096]{2,1,0:T(4,128)(2,1)}, bf16[4,4,4096]{2,1,0:T(4,128)(2,1)S(1)}, u32[]{:S(2)}, u32[]{:S(2)}) collective-permute-start(bf16[4,4,4096]{2,1,0:T(4,128)(2,1)} %param.12), channel_id=1, source_target_pairs={{0,16},{16,32},{32,48},{48,64},{64,80},{80,96},{96,112},{112,128},... | collective-permute-start | bytes 393224 | tf_op jit(solution)/shard_map/ppermute | solution.py:20
  18.3 17.8 %collective-permute-start.1 = (bf16[4,4,4096]{2,1,0:T(4,128)(2,1)}, bf16[4,4,4096]{2,1,0:T(4,128)(2,1)S(1)}, u32[]{:S(2)}, u32[]{:S(2)}) collective-permute-start(bf16[4,4,4096]{2,1,0:T(4,128)(2,1)} %param.12), channel_id=1, source_target_pairs={{16,0},{32,16},{48,32},{64,48},{80,64},{96,80},{112,96},{128,112},... | collective-permute-start | bytes 393224 | tf_op jit(solution)/shard_map/ppermute | solution.py:20
  23.2 6.8 %copy-start.4 = (f32[64]{0:T(128)S(1)}, f32[64]{0:T(128)}, u32[]{:S(2)}) copy-start(f32[64]{0:T(128)} %param.15) | copy-start | bytes 772
  23.2 6.8 %copy-start.1 = (bf16[4,4,4096]{2,1,0:T(4,128)(2,1)S(1)}, bf16[4,4,4096]{2,1,0:T(4,128)(2,1)}, u32[]{:S(2)}) copy-start(bf16[4,4,4096]{2,1,0:T(4,128)(2,1)} %param.12) | copy-start | bytes 393220
  101.2 83.8 %copy-start = (bf16[4,4,3,256,128]{4,3,2,1,0:T(8,128)(2,1)S(1)}, bf16[4,4,3,256,128]{4,3,2,1,0:T(8,128)(2,1)}, u32[]{:S(2)}) copy-start(bf16[4,4,3,256,128]{4,3,2,1,0:T(8,128)(2,1)} %get-tuple-element.11) | copy-start | bytes 9437188
  188.8 1.0 copy-start.2
  188.8 1.2 copy-start.3
  188.8 1.2 copy-start.5
  188.8 1.3 copy-start.6
Sparse Core Ops, SparseCore 0:
  9.2 60.0 all-gather.1
  81.4 103.6 all-reduce.1
where the time goes:
time: 199 us
  waiting for transfers between devices  112 us (56%)
  matrix products  32.4 us (16%)
  local copies, waits for them, and re-layouts  22.8 us (11%)
  between operations  13.6 us (7%)
  starting transfers between devices  11.3 us (6%)
  other arithmetic  6.46 us (3%)
    psum x1, waiting for transfers between devices, from_root(): return lax.psum(kept, axis)  82.1 us
    all_gather x1, waiting for transfers between devices, on_device(): piece = lax.all_gather(fitting, 'col', axis=0, tiled=True)  29.6 us
    dot_general x1, matrix products, on_device(): jnp.einsum('ism,map->isap', picker, piece, preferred_element_type=jnp.flo...  12 us
    ppermute x4, starting transfers between devices, passed_along(): return lax.ppermute(block, axis, route)  11.3 us
    slice x1, local copies, waits for them, and re-layouts, on_device(): coefficients[:, :, domain_size:]  6.75 us
    dot_general x1, matrix products, on_device(): jnp.einsum('ijnac,ijndc->ijnad', half, intersection_mats, preferred_eleme...  5.3 us
    dot_general x1, matrix products, on_device(): jnp.einsum('isap,ijspq->ijsaq', row_fit, coefficients[:, :, :domain_size]...  4.82 us
  transfers between devices with their start and end apart: 6, of which 2 were waited for; matrix products, arithmetic and copies ran while one was open for 21% of the time, Pallas kernels for 0%

commit v1 on v0

--- a/solution.py
+++ b/solution.py
@@ -43,7 +43,9 @@
     wanted = (
         lax.dynamic_slice_in_dim(orbital_atoms, first_row, row_count, 0) - row_place * row_atoms
     )
-    piece = lax.all_gather(fitting, "col", axis=0, tiled=True)
+    piece = jnp.concatenate(
+        lax.all_to_all(jnp.stack([fitting] * lax.axis_size("col")), "col", 0, 0), axis=0
+    )
     labels = jnp.arange(piece.shape[0], dtype=jnp.int32)
     picker = (wanted[:, :, None] == labels[None, None, :]).astype(jnp.bfloat16)
     added = jnp.einsum("ism,map->isap", picker, piece, preferred_element_type=jnp.float32)

time: 199 us -> 368 us (1.85)
  waiting for transfers between devices: 112 us -> 246 us
  local copies, waits for them, and re-layouts: 22.8 us -> 54 us
  starting transfers between devices: 11.3 us -> 20 us
    ppermute x4, waiting for transfers between devices: 0.01 us -> 162 us  [passed_along(): return lax.ppermute(block, axis, route)]
    all_gather x1 -> x0, waiting for transfers between devices: 29.6 us -> none  [on_device(): piece = lax.all_gather(fitting, 'col', axis=0, tiled=True)]
    reshape x0 -> x1, local copies, waits for them, and re-layouts: none -> 13.1 us  [on_device(): jnp.concatenate(lax.all_to_all(jnp.stack([fitting] * lax.axis_size('col')...]
    all_to_all x0 -> x1, local copies, waits for them, and re-layouts: none -> 10.9 us  [on_device(): lax.all_to_all(jnp.stack([fitting] * lax.axis_size('col')), 'col', 0, 0)]
    all_to_all x0 -> x1, starting transfers between devices: none -> 10.1 us  [on_device(): lax.all_to_all(jnp.stack([fitting] * lax.axis_size('col')), 'col', 0, 0)]
    another operation x0 -> x1, local copies, waits for them, and re-layouts: none -> 7.61 us  [on_device(): jnp.stack([fitting] * lax.axis_size('col'))]
  transfers between devices with their start and end apart: 6 -> 6, of which waited for: 2 -> 3; matrix products, arithmetic and copies ran while one was open for 21% -> 11% of each run, Pallas kernels for 0% -> 0%
where the time goes in v1:
time: 368 us; the launch traced here: 367 us
  waiting for transfers between devices  246 us (67%)
  local copies, waits for them, and re-layouts  54 us (15%)
  matrix products  29.5 us (8%)
  starting transfers between devices  20 us (5%)
  between operations  13.6 us (4%)
  other arithmetic  4.34 us (1%)
    ppermute x4, waiting for transfers between devices, passed_along(): return lax.ppermute(block, axis, route)  162 us
    psum x1, waiting for transfers between devices, from_root(): return lax.psum(kept, axis)  83.6 us
    reshape x1, local copies, waits for them, and re-layouts, on_device(): jnp.concatenate(lax.all_to_all(jnp.stack([fitting] * lax.axis_size('col')...  13.1 us
    all_to_all x1, local copies, waits for them, and re-layouts, on_device(): lax.all_to_all(jnp.stack([fitting] * lax.axis_size('col')), 'col', 0, 0)  10.9 us
    all_to_all x1, starting transfers between devices, on_device(): lax.all_to_all(jnp.stack([fitting] * lax.axis_size('col')), 'col', 0, 0)  10.1 us
    ppermute x4, starting transfers between devices, passed_along(): return lax.ppermute(block, axis, route)  9.88 us
    dot_general x1, matrix products, on_device(): jnp.einsum('ism,map->isap', picker, piece, preferred_element_type=jnp.flo...  8.78 us
    another operation x1, local copies, waits for them, and re-layouts, on_device(): jnp.stack([fitting] * lax.axis_size('col'))  7.61 us
  transfers between devices with their start and end apart: 6, of which 3 were waited for; matrix products, arithmetic and copies ran while one was open for 11% of the time, Pallas kernels for 0%

profile of v1, /device:TPU:1, one launch (start us, length us, event | category | flops | bytes accessed | tf_op | source)
XLA Modules:
  0.0 367.1 jit_solution(14670217610529385509)
XLA Ops:
  6.5 1.6 copy.68
  8.1 7.6 %stack.2 = bf16[16,2,512,256]{3,1,2,0:T(2,128)(2,1)} broadcast(bf16[2,512,256]{2,0,1:T(2,128)(2,1)S(1)} %copy.68), dimensions={1,2,3} | broadcast | bytes 8912896 | tf_op jit(solution)/shard_map/stack | solution.py:47
  15.8 10.1 %all-to-all-start = ((bf16[16,2,512,256]{3,1,2,0:T(2,128)(2,1)}), bf16[16,2,512,256]{3,1,2,0:T(2,128)(2,1)}, u32[]{:S(2)}, u32[]{:S(2)}) async-start(bf16[16,2,512,256]{3,1,2,0:T(2,128)(2,1)} %stack.2), calls=%async_computation | async-start | bytes 16777216 | tf_op jit(solution)/shard_map/all_to_all | solution.py:47
  25.9 0.1 copy.84
  26.0 3.5 collective-permute-start.2
  29.6 1.9 collective-permute-start.3
  31.5 3.1 collective-permute-start
  34.6 1.3 collective-permute-start.1
  36.0 0.1 compare_and_fusion.1
  36.0 0.1 copy.87
  36.1 0.1 reshape.64
  36.2 0.1 copy.81
  36.3 0.1 reshape.56
  36.5 0.1 constant_dynamic-slice_fusion.1
  36.7 6.3 %fusion.57 = (bf16[4,4,3,256,128]{4,3,2,1,0:T(8,128)(2,1)}, bf16[4,4,3,256,128]{4,3,2,1,0:T(8,128)(2,1)}) fusion(bf16[4,4,6,256,128]{4,3,2,1,0:T(8,128)(2,1)} %param.11), kind=kLoop, calls=%fused_computation.50 | loop fusion | bytes 12582912 | tf_op jit(solution)/shard_map/slice | solution.py:64
  43.0 0.1 fusion.59
  43.1 1.0 reshape.53
  44.1 0.1 copy.83
  44.2 0.1 copy.80
  44.3 3.3 reshape.51
  47.6 0.1 copy.78
  47.7 0.1 copy.79
  47.8 0.1 pad_maximum_fusion.3
  47.9 160.1 %collective-permute-done.2 = bf16[4,4,4096]{2,0,1:T(4,128)(2,1)S(1)} collective-permute-done((bf16[4,4,4096]{2,0,1:T(4,128)(2,1)S(1)}, bf16[4,4,4096]{2,0,1:T(4,128)(2,1)S(1)}, u32[]{:S(2)}, u32[]{:S(2)}) %collective-permute-start.2) | collective-permute-done | bytes 131104 | tf_op jit(solution)/shard_map/ppermute | solution.py:20
  208.0 1.9 collective-permute-done.3
  209.8 0.3 pad_maximum_fusion.2
  210.1 1.0 gather_fusion.1
  211.1 0.3 pad_maximum_fusion.1
  211.4 1.8 gather_fusion
  213.2 1.5 fusion.51
  214.7 10.9 %copy.69 = bf16[16,2,512,256]{3,1,0,2:T(2,128)(2,1)} copy(bf16[16,2,512,256]{3,1,2,0:T(2,128)(2,1)} %all-to-all-done) | data formatting | bytes 16777216 | tf_op jit(solution)/shard_map/all_to_all | solution.py:47
  225.6 13.1 %reshape.75 = bf16[32,512,256,1]{2,0,1,3:T(8,128)(2,1)} reshape(bf16[16,2,512,256]{3,1,0,2:T(2,128)(2,1)} %copy.69) | data formatting | bytes 16777216 | tf_op jit(solution)/shard_map/reshape | solution.py:46
  238.7 8.8 %broadcast_select_fusion = (bf16[4,3,512,256]{3,0,2,1:T(4,128)(2,1)}, bf16[4,3,512,256]{3,0,2,1:T(4,128)(2,1)}) fusion(pred[]{:T(512)S(6)} %eq.19, bf16[32,512,256,1]{2,0,1,3:T(8,128)(2,1)} %reshape.75, s32[4,3]{0,1:T(4,128)S(1)} %dynamic-slice_subtract_fusion), kind=kOutput, calls=%fused_computation.16 | convolution fusion | flops 103809408 | bytes 14680113 | tf_op jit(solution)/shard_map/ism,map->isap/dot_general | solution.py:51
  247.5 2.0 pad_maximum_fusion
  249.5 3.3 reshape.50
  252.8 5.3 %fusion.12 = bf16[4,4,8,64,64]{4,3,2,1,0:T(8,128)(2,1)} fusion(bf16[4,4,8,64,64]{4,3,2,1,0:T(8,128)(2,1)S(1)} %reshape.51, bf16[4,4,8,64,64]{4,3,2,1,0:T(8,128)(2,1)} %reshape.50), kind=kOutput, calls=%fused_computation.18 | convolution fusion | flops 134742016 | bytes 3145728 | tf_op jit(solution)/shard_map/ijnac,ijndc->ijnad/dot_general | solution.py:99
  258.0 4.2 %fusion = f32[4,4,1,64,64]{4,2,3,1,0:T(1,128)} fusion(f32[4,4,8,1,1]{2,3,4,1,0:T(1,128)S(1)} %bitcast.60, bf16[4,4,8,64,64]{4,3,2,1,0:T(8,128)(2,1)} %fusion.12), kind=kOutput, calls=%fused_computation.4 | convolution fusion | flops 1048576 | bytes 1311232 | tf_op jit(solution)/shard_map/ijn,ijnad->ijad/dot_general | solution.py:111
  262.3 4.8 %convert_bitcast_fusion.1 = bf16[4,4,3,512,128]{3,4,1,2,0:T(8,128)(2,1)S(1)} fusion(bf16[4,4,3,256,128]{4,3,2,1,0:T(8,128)(2,1)} %get-tuple-element.12, bf16[4,3,512,256,1]{3,0,2,1,4:T(4,128)(2,1)} %bitcast.55), kind=kOutput, calls=%fused_computation.3 | convolution fusion | flops 1613758464 | bytes 12582912 | tf_op jit(solution)/shard_map/isap,ijspq->ijsaq/dot_general | solution.py:55
  267.1 0.8 fusion.58
  267.9 1.8 fusion.16
  269.6 83.6 %all-reduce.2.cloned.1.call-done = bf16[4,3,512,256]{3,0,2,1:T(4,128)(2,1)} async-done(((bf16[4,3,512,256]{3,0,2,1:T(4,128)(2,1)}), bf16[4,3,512,256]{3,0,2,1:T(4,128)(2,1)}) %all-reduce.2.cloned.1.call-update) | async-done | bytes 3145744 | tf_op jit(solution)/shard_map/psum | solution.py:14
  353.2 3.7 %convert_bitcast_fusion = bf16[4,4,3,512,128]{3,4,0,2,1:T(8,128)(2,1)S(1)} fusion(bf16[4,4,3,256,128]{4,3,2,1,0:T(8,128)(2,1)S(1)} %copy-done, bf16[4,3,512,256,1]{3,0,2,1,4:T(4,128)(2,1)} %bitcast.56), kind=kOutput, calls=%fused_computation.2 | convolution fusion | flops 1613758464 | bytes 12582912 | tf_op jit(solution)/shard_map/jsap,ijspq->ijsaq/dot_general | solution.py:61
  357.0 0.4 fusion.56
  357.5 0.5 copy-done.2
  358.0 0.2 copy-done.3
  358.2 0.2 copy-done.10
  358.4 1.0 fusion.46
  359.4 0.9 reshape.52
  (30 shorter events, 0.3 us)
Async XLA Ops:
  15.7 10.2 %copy-start.1 = (bf16[4,4,4096]{2,1,0:T(4,128)(2,1)S(1)}, bf16[4,4,4096]{2,1,0:T(4,128)(2,1)}, u32[]{:S(2)}) copy-start(bf16[4,4,4096]{2,1,0:T(4,128)(2,1)} %param.12) | copy-start | bytes 393220
  15.7 20.2 %copy-start.5 = (s32[64,4]{0,1:T(4,128)S(1)}, s32[64,4]{0,1:T(4,128)}, u32[]{:S(2)}) copy-start(s32[64,4]{0,1:T(4,128)} %param.18) | copy-start | bytes 3076
  15.7 20.7 %copy-start.7 = (s32[64,3]{0,1:T(4,128)S(1)}, s32[64,3]{0,1:T(4,128)}, u32[]{:S(2)}) copy-start(s32[64,3]{0,1:T(4,128)} %param.17) | copy-start | bytes 2308
  15.7 20.8 %copy-start.4 = (f32[64,4]{0,1:T(4,128)S(1)}, f32[64,4]{0,1:T(4,128)}, u32[]{:S(2)}) copy-start(f32[64,4]{0,1:T(4,128)} %param.19) | copy-start | bytes 3076
  15.7 20.8 %copy-start.8 = (s32[4,4]{1,0:T(4,128)S(1)}, s32[4,4]{1,0:T(4,128)}, u32[]{:S(2)}) copy-start(s32[4,4]{1,0:T(4,128)} %param.16) | copy-start | bytes 196
  15.8 198.9 %all-to-all-start = ((bf16[16,2,512,256]{3,1,2,0:T(2,128)(2,1)}), bf16[16,2,512,256]{3,1,2,0:T(2,128)(2,1)}, u32[]{:S(2)}, u32[]{:S(2)}) async-start(bf16[16,2,512,256]{3,1,2,0:T(2,128)(2,1)} %stack.2), calls=%async_computation | async-start | bytes 16777216 | tf_op jit(solution)/shard_map/all_to_all | solution.py:47
  25.9 327.4 %all-reduce.2.cloned.1.call-start = ((), (), s32[]{:S(2)}) async-start(), calls=%async_computation.1 | async-start | bytes 6291456 | tf_op jit(solution)/shard_map/psum | solution.py:14
  26.0 181.9 %collective-permute-start.2 = (bf16[4,4,4096]{2,0,1:T(4,128)(2,1)S(1)}, bf16[4,4,4096]{2,0,1:T(4,128)(2,1)S(1)}, u32[]{:S(2)}, u32[]{:S(2)}) collective-permute-start(bf16[4,4,4096]{2,0,1:T(4,128)(2,1)S(1)} %copy.84), channel_id=1, source_target_pairs={{0,1},{1,2},{2,3},{3,4},{4,5},{5,6},{6,7},{7,8},{8,9},{9,10},{10,1... | collective-permute-start | bytes 393224 | tf_op jit(solution)/shard_map/ppermute | solution.py:20
  29.6 180.3 %collective-permute-start.3 = (bf16[4,4,4096]{2,0,1:T(4,128)(2,1)S(1)}, bf16[4,4,4096]{2,0,1:T(4,128)(2,1)S(1)}, u32[]{:S(2)}, u32[]{:S(2)}) collective-permute-start(bf16[4,4,4096]{2,0,1:T(4,128)(2,1)S(1)} %copy.84), channel_id=1, source_target_pairs={{1,0},{2,1},{3,2},{4,3},{5,4},{6,5},{7,6},{8,7},{9,8},{10,9},{11,1... | collective-permute-start | bytes 393224 | tf_op jit(solution)/shard_map/ppermute | solution.py:20
  31.5 179.6 %collective-permute-start = (bf16[4,4,4096]{2,1,0:T(4,128)(2,1)S(1)}, bf16[4,4,4096]{2,1,0:T(4,128)(2,1)S(1)}, u32[]{:S(2)}, u32[]{:S(2)}) collective-permute-start(bf16[4,4,4096]{2,1,0:T(4,128)(2,1)S(1)} %copy-done.1), channel_id=1, source_target_pairs={{0,16},{16,32},{32,48},{48,64},{64,80},{80,96},{96,112},{112,128},... | collective-permute-start | bytes 393224 | tf_op jit(solution)/shard_map/ppermute | solution.py:20
  34.6 176.5 %collective-permute-start.1 = (bf16[4,4,4096]{2,1,0:T(4,128)(2,1)S(1)}, bf16[4,4,4096]{2,1,0:T(4,128)(2,1)S(1)}, u32[]{:S(2)}, u32[]{:S(2)}) collective-permute-start(bf16[4,4,4096]{2,1,0:T(4,128)(2,1)S(1)} %copy-done.1), channel_id=1, source_target_pairs={{16,0},{32,16},{48,32},{64,48},{80,64},{96,80},{112,96},{128,112},... | collective-permute-start | bytes 393224 | tf_op jit(solution)/shard_map/ppermute | solution.py:20
  36.7 6.3 %copy-start.6 = (f32[64]{0:T(128)S(1)}, f32[64]{0:T(128)}, u32[]{:S(2)}) copy-start(f32[64]{0:T(128)} %param.15) | copy-start | bytes 772
  267.9 85.4 %copy-start = (bf16[4,4,3,256,128]{4,3,2,1,0:T(8,128)(2,1)S(1)}, bf16[4,4,3,256,128]{4,3,2,1,0:T(8,128)(2,1)}, u32[]{:S(2)}) copy-start(bf16[4,4,3,256,128]{4,3,2,1,0:T(8,128)(2,1)} %get-tuple-element.11) | copy-start | bytes 9437188
  357.0 1.0 copy-start.2
  357.0 1.2 copy-start.3
  357.0 1.2 copy-start.9
  357.0 1.3 copy-start.10
Sparse Core Ops, SparseCore 0:
  247.6 105.5 all-reduce.1
